TPU v7x, 32 devices: a whole 2x2x4 slice. The times are simulated.
32 devices in a mesh: slab: 8 (over z, core), cross: 4 (over y, x).
Axes of the slice: x: 2, y: 2, z: 4, core: 2. Of those that a mesh axis runs over, the one named last changes fastest.
Arguments:
- forcing: float32 [2, 32, 256, 512], P(None, 'slab', 'cross'), may hold values from -6 to 6
- viscosity: float32 [32, 256, 512], P('slab', 'cross'), may hold values from 0.1 to 10
- owner_slot: int32 [512], replicated, may hold values from 0 to 511, each once
Outputs:
- velocity: float32 [2, 32, 256, 512], P(None, 'slab', 'cross')
- pressure: float32 [32, 512], P('slab', 'cross')
All inputs are finite; a program needn't handle non-finite values.
Results may differ from a plain program's by a relative error of at most 0.00013.
Values sent between devices are 32-bit elements; how exact they have to be, the bound alone decides.
A program may use at most 64 MiB of HBM per device.

v0:
```python
import jax
import jax.numpy as jnp
from jax import lax
from jax.sharding import PartitionSpec as P

OUTER = 2
DEGREE = 3
cheb_theta = 1.025
cheb_delta = 0.975


def with_halo(cells, sides, width):
    for axis, dim in sides:
        count = lax.axis_size(axis)
        ends = count - 1
        head = lax.slice_in_dim(cells, 0, width, axis=dim)
        tail = lax.slice_in_dim(cells, cells.shape[dim] - width, cells.shape[dim], axis=dim)
        cells = jnp.concatenate(
            [
                lax.ppermute(tail, axis, [(i, (i + 1) % count) for i in range(ends)]),
                cells,
                lax.ppermute(head, axis, [((i + 1) % count, i) for i in range(ends)]),
            ],
            axis=dim,
        )
    return cells


def passed_along(block, axis, distance):
    devices = range(lax.axis_size(axis))
    route = [(i - distance, i) for i in devices if i - distance in devices]
    return lax.ppermute(block, axis, route)


def face_parts(viscosity):
    rim = with_halo(viscosity, (("slab", 0), ("cross", 1)), 1)
    rim = jnp.pad(rim, ((0, 0), (0, 0), (1, 1)))
    centre = rim[1:-1, 1:-1, 1:-1]
    neighbours = [
        rim[2:, 1:-1, 1:-1],
        rim[:-2, 1:-1, 1:-1],
        rim[1:-1, 2:, 1:-1],
        rim[1:-1, :-2, 1:-1],
        rim[1:-1, 1:-1, 2:],
        rim[1:-1, 1:-1, :-2],
    ]
    faces = [0.5 * (centre + nb) for nb in neighbours]
    diag = faces[0] + faces[1] + faces[2] + faces[3] + faces[4] + faces[5]
    return (faces, diag)


def apply_op(field, faces):
    padded = with_halo(field, (("slab", 1), ("cross", 2)), 1)
    padded = jnp.pad(padded, ((0, 0), (0, 0), (0, 0), (1, 1)))
    neighbours = [
        padded[:, 2:, 1:-1, 1:-1],
        padded[:, :-2, 1:-1, 1:-1],
        padded[:, 1:-1, 2:, 1:-1],
        padded[:, 1:-1, :-2, 1:-1],
        padded[:, 1:-1, 1:-1, 2:],
        padded[:, 1:-1, 1:-1, :-2],
    ]
    result = jnp.zeros_like(field)
    for face, nb in zip(faces, neighbours):
        result = result + face[None] * (field - nb)
    return result


def velocity_solve(rhs, faces, diag):
    sigma = cheb_theta / cheb_delta
    solved = rhs / (cheb_theta * diag[None])
    change = solved
    rho_prev = 1.0 / sigma
    for step in range(DEGREE - 1):
        resid = rhs - apply_op(solved, faces)
        rho = 1.0 / (2.0 * sigma - rho_prev)
        change = rho * rho_prev * change + 2.0 * rho / cheb_delta * resid / diag[None]
        solved = solved + change
        rho_prev = rho
    return solved


def diverge(field, onehot):
    col_x = jnp.sum(field[0], axis=1)
    col_z = jnp.sum(field[1], axis=1)
    prior = passed_along(col_x[-1:], "slab", 1)
    below = jnp.concatenate([prior, col_x[:-1]], 0)
    behind = jnp.pad(col_z[:, :-1], ((0, 0), (1, 0)))
    local = col_x - below + col_z - behind
    ordered = jnp.dot(local, onehot, precision=lax.Precision.HIGHEST)
    return lax.psum(ordered, "cross")


def gradient(press, onehot, ny):
    column = jnp.dot(press, onehot.T, precision=lax.Precision.HIGHEST)
    after = passed_along(column[:1], "slab", -1)
    grad_x = column - jnp.concatenate([column[1:], after], 0)
    grad_z = column - jnp.pad(column[:, 1:], ((0, 0), (0, 1)))
    both = jnp.stack([grad_x, grad_z])[:, :, None, :]
    return jnp.broadcast_to(both, (2, column.shape[0], ny, column.shape[1]))


def total(value):
    return lax.psum(value, "slab")


def shards(forcing, viscosity, owner_slot):
    faces, diag = face_parts(viscosity)
    ny = viscosity.shape[1]
    depth = owner_slot.shape[0]
    onehot = (owner_slot[:, None] == jnp.arange(depth, dtype=jnp.int32)[None, :]).astype(
        jnp.float32
    )
    target = diverge(velocity_solve(forcing, faces, diag), onehot)
    pressure = jnp.zeros_like(target)
    resid = target
    dirn = target
    rr = total(jnp.sum(resid * resid))
    for step in range(OUTER):
        image = diverge(velocity_solve(gradient(dirn, onehot, ny), faces, diag), onehot)
        alpha = rr / total(jnp.sum(dirn * image))
        pressure = pressure + alpha * dirn
        if step + 1 < OUTER:
            resid = resid - alpha * image
            fresh = total(jnp.sum(resid * resid))
            dirn = resid + fresh / rr * dirn
            rr = fresh
    velocity = velocity_solve(forcing - gradient(pressure, onehot, ny), faces, diag)
    width = depth // lax.axis_size("cross")
    owned_cols = lax.dynamic_slice_in_dim(pressure, lax.axis_index("cross") * width, width, 1)
    return (velocity, owned_cols)


def solution(mesh):
    in_specs = (P(None, "slab", "cross", None), P("slab", "cross", None), P())
    out_specs = (P(None, "slab", "cross", None), P("slab", "cross"))
    return jax.shard_map(shards, mesh=mesh, in_specs=in_specs, out_specs=out_specs, check_vma=False)
```

profile of v0, /device:TPU:12, one launch (start us, length us, event | category | flops | bytes accessed | tf_op | source)
XLA Modules:
  0.0 310.1 jit_solution(14923868998203583419)
XLA Ops:
  3.6 3.6 %collective-permute-start = (f32[1,64,512]{2,1,0:T(8,128)S(1)}, f32[1,64,512]{2,1,0:T(8,128)S(1)}, u32[]{:S(2)}, u32[]{:S(2)}) collective-permute-start(f32[1,64,512]{2,1,0:T(8,128)S(1)} %get-tuple-element.62), channel_id=1, source_target_pairs={{4,0},{8,4},{12,8},{16,12},{20,16},{24,20},{28,24},{5,1},{9,5},{13... | collective-permute-start | bytes 393224 | tf_op jit(solution)/shard_map/ppermute | solution.py:22
  15.7 4.0 %collective-permute-done.3 = f32[6,1,512]{2,1,0:T(1,128)S(1)} collective-permute-done((f32[6,1,512]{2,1,0:T(1,128)S(1)}, f32[6,1,512]{2,1,0:T(1,128)S(1)}, u32[]{:S(2)}, u32[]{:S(2)}) %collective-permute-start.3) | collective-permute-done | bytes 12320 | tf_op jit(solution)/shard_map/ppermute | solution.py:20
  28.7 3.8 %collective-permute-done.5 = f32[2,1,64,512]{3,2,1,0:T(8,128)S(1)} collective-permute-done((f32[2,1,64,512]{3,2,1,0:T(8,128)S(1)}, f32[2,1,64,512]{3,2,1,0:T(8,128)S(1)}, u32[]{:S(2)}, u32[]{:S(2)}) %collective-permute-start.5) | collective-permute-done | bytes 262176 | tf_op jit(solution)/shard_map/ppermute | solution.py:20
  34.5 3.9 %collective-permute-start.7 = (f32[2,6,1,512]{3,2,1,0:T(1,128)S(1)}, f32[2,6,1,512]{3,2,1,0:T(1,128)S(1)}, u32[]{:S(2)}, u32[]{:S(2)}) collective-permute-start(f32[2,6,1,512]{3,2,1,0:T(1,128)S(1)} %get-tuple-element.42), channel_id=1, source_target_pairs={{0,1},{1,2},{2,3},{4,5},{5,6},{6,7},{8,9},{9,10},{10,11},{12,13},{... | collective-permute-start | bytes 73736 | tf_op jit(solution)/shard_map/ppermute | solution.py:20
  49.4 3.8 %collective-permute-done.9 = f32[2,1,64,512]{3,2,1,0:T(8,128)S(1)} collective-permute-done((f32[2,1,64,512]{3,2,1,0:T(8,128)S(1)}, f32[2,1,64,512]{3,2,1,0:T(8,128)S(1)}, u32[]{:S(2)}, u32[]{:S(2)}) %collective-permute-start.9) | collective-permute-done | bytes 262176 | tf_op jit(solution)/shard_map/ppermute | solution.py:20
  55.2 3.9 %collective-permute-start.11 = (f32[2,6,1,512]{3,2,1,0:T(1,128)S(1)}, f32[2,6,1,512]{3,2,1,0:T(1,128)S(1)}, u32[]{:S(2)}, u32[]{:S(2)}) collective-permute-start(f32[2,6,1,512]{3,2,1,0:T(1,128)S(1)} %get-tuple-element.40), channel_id=1, source_target_pairs={{0,1},{1,2},{2,3},{4,5},{5,6},{6,7},{8,9},{9,10},{10,11},{12,13},{... | collective-permute-start | bytes 73736 | tf_op jit(solution)/shard_map/ppermute | solution.py:20
  70.0 8.7 %psum.49 = f32[4,512]{1,0:T(4,128)S(1)} all-reduce(f32[4,512]{1,0:T(4,128)S(1)} %fusion.163), channel_id=1, replica_groups=mesh['slab'=8,'cross'=4] {'cross'}, use_global_device_ids=true, to_apply=%region_2.3 | all-reduce | flops 2048 | bytes 16384 | tf_op jit(solution)/shard_map/psum | solution.py:91
  91.3 3.8 %collective-permute-done.15 = f32[2,1,64,512]{3,2,1,0:T(8,128)S(1)} collective-permute-done((f32[2,1,64,512]{3,2,1,0:T(8,128)S(1)}, f32[2,1,64,512]{3,2,1,0:T(8,128)S(1)}, u32[]{:S(2)}, u32[]{:S(2)}) %collective-permute-start.15) | collective-permute-done | bytes 262176 | tf_op jit(solution)/shard_map/ppermute | solution.py:20
  113.0 3.8 %collective-permute-done.19 = f32[2,1,64,512]{3,2,1,0:T(8,128)S(1)} collective-permute-done((f32[2,1,64,512]{3,2,1,0:T(8,128)S(1)}, f32[2,1,64,512]{3,2,1,0:T(8,128)S(1)}, u32[]{:S(2)}, u32[]{:S(2)}) %collective-permute-start.19) | collective-permute-done | bytes 262176 | tf_op jit(solution)/shard_map/ppermute | solution.py:20
  122.8 3.8 %collective-permute-done.21 = f32[2,6,1,512]{3,2,1,0:T(1,128)S(1)} collective-permute-done((f32[2,6,1,512]{3,2,1,0:T(1,128)S(1)}, f32[2,6,1,512]{3,2,1,0:T(1,128)S(1)}, u32[]{:S(2)}, u32[]{:S(2)}) %collective-permute-start.21) | collective-permute-done | bytes 24608 | tf_op jit(solution)/shard_map/ppermute | solution.py:20
  134.6 7.7 %psum.51 = f32[4,512]{1,0:T(4,128)S(1)} all-reduce(f32[4,512]{1,0:T(4,128)S(1)} %fusion.161), channel_id=1, replica_groups=mesh['slab'=8,'cross'=4] {'cross'}, use_global_device_ids=true, to_apply=%region_7.8 | all-reduce | flops 2048 | bytes 16384 | tf_op jit(solution)/shard_map/psum | solution.py:91
  143.0 10.6 %all-reduce.15 = (f32[]{:T(128)}, f32[]{:T(128)}) all-reduce(f32[]{:T(128)} %get-tuple-element.9, f32[]{:T(128)} %get-tuple-element.8), channel_id=1, replica_groups=mesh['slab'=8,'cross'=4] {'slab'}, use_global_device_ids=true, to_apply=%region_4.5 | all-reduce | flops 2 | bytes 16 | tf_op jit(solution)/shard_map/psum | solution.py:104
  155.5 14.3 %psum.53 = f32[]{:T(128)} all-reduce(f32[]{:T(128)} %multiply_reduce_fusion.1), channel_id=1, replica_groups=mesh['slab'=8,'cross'=4] {'slab'}, use_global_device_ids=true, to_apply=%region_11.12 | all-reduce | flops 1 | bytes 8 | tf_op jit(solution)/shard_map/psum | solution.py:104
  171.7 5.0 %collective-permute-start.23 = (f32[1,512]{1,0:T(1,128)S(1)}, f32[1,512]{1,0:T(1,128)S(1)}, u32[]{:S(2)}, u32[]{:S(2)}) collective-permute-start(f32[1,512]{1,0:T(1,128)S(1)} %slice.583), channel_id=1, source_target_pairs={{4,0},{8,4},{12,8},{16,12},{20,16},{24,20},{28,24},{5,1},{9,5},{13... | collective-permute-start | bytes 6152 | tf_op jit(solution)/shard_map/ppermute | solution.py:32
  186.7 3.8 %collective-permute-done.25 = f32[2,1,64,512]{3,2,1,0:T(8,128)S(1)} collective-permute-done((f32[2,1,64,512]{3,2,1,0:T(8,128)S(1)}, f32[2,1,64,512]{3,2,1,0:T(8,128)S(1)}, u32[]{:S(2)}, u32[]{:S(2)}) %collective-permute-start.25) | collective-permute-done | bytes 262176 | tf_op jit(solution)/shard_map/ppermute | solution.py:20
  190.6 4.1 %collective-permute-start.26 = (f32[2,6,1,512]{3,2,1,0:T(1,128)S(1)}, f32[2,6,1,512]{3,2,1,0:T(1,128)S(1)}, u32[]{:S(2)}, u32[]{:S(2)}) collective-permute-start(f32[2,6,1,512]{3,2,1,0:T(1,128)S(1)} %get-tuple-element.35), channel_id=1, source_target_pairs={{1,0},{2,1},{3,2},{5,4},{6,5},{7,6},{9,8},{10,9},{11,10},{13,12},{... | collective-permute-start | bytes 73736 | tf_op jit(solution)/shard_map/ppermute | solution.py:22
  196.6 4.7 %collective-permute-done.27 = f32[2,6,1,512]{3,2,1,0:T(1,128)S(1)} collective-permute-done((f32[2,6,1,512]{3,2,1,0:T(1,128)S(1)}, f32[2,6,1,512]{3,2,1,0:T(1,128)S(1)}, u32[]{:S(2)}, u32[]{:S(2)}) %collective-permute-start.27) | collective-permute-done | bytes 24608 | tf_op jit(solution)/shard_map/ppermute | solution.py:20
  209.6 3.8 %collective-permute-done.29 = f32[2,1,64,512]{3,2,1,0:T(8,128)S(1)} collective-permute-done((f32[2,1,64,512]{3,2,1,0:T(8,128)S(1)}, f32[2,1,64,512]{3,2,1,0:T(8,128)S(1)}, u32[]{:S(2)}, u32[]{:S(2)}) %collective-permute-start.29) | collective-permute-done | bytes 262176 | tf_op jit(solution)/shard_map/ppermute | solution.py:20
  215.5 3.8 %collective-permute-start.31 = (f32[2,6,1,512]{3,2,1,0:T(1,128)S(1)}, f32[2,6,1,512]{3,2,1,0:T(1,128)S(1)}, u32[]{:S(2)}, u32[]{:S(2)}) collective-permute-start(f32[2,6,1,512]{3,2,1,0:T(1,128)S(1)} %get-tuple-element.32), channel_id=1, source_target_pairs={{0,1},{1,2},{2,3},{4,5},{5,6},{6,7},{8,9},{9,10},{10,11},{12,13},{... | collective-permute-start | bytes 73736 | tf_op jit(solution)/shard_map/ppermute | solution.py:20
  230.1 8.6 %psum.54 = f32[4,512]{1,0:T(4,128)S(1)} all-reduce(f32[4,512]{1,0:T(4,128)S(1)} %fusion.159), channel_id=1, replica_groups=mesh['slab'=8,'cross'=4] {'cross'}, use_global_device_ids=true, to_apply=%region_14.15 | all-reduce | flops 2048 | bytes 16384 | tf_op jit(solution)/shard_map/psum | solution.py:91
  239.4 11.2 %psum.55 = f32[]{:T(128)} all-reduce(f32[]{:T(128)} %multiply_reduce_fusion), channel_id=1, replica_groups=mesh['slab'=8,'cross'=4] {'slab'}, use_global_device_ids=true, to_apply=%region_16.17 | all-reduce | flops 1 | bytes 8 | tf_op jit(solution)/shard_map/psum | solution.py:104
  265.4 3.8 %collective-permute-done.35 = f32[2,1,64,512]{3,2,1,0:T(8,128)S(1)} collective-permute-done((f32[2,1,64,512]{3,2,1,0:T(8,128)S(1)}, f32[2,1,64,512]{3,2,1,0:T(8,128)S(1)}, u32[]{:S(2)}, u32[]{:S(2)}) %collective-permute-start.35) | collective-permute-done | bytes 262176 | tf_op jit(solution)/shard_map/ppermute | solution.py:20
  275.3 3.7 %collective-permute-done.37 = f32[2,6,1,512]{3,2,1,0:T(1,128)S(1)} collective-permute-done((f32[2,6,1,512]{3,2,1,0:T(1,128)S(1)}, f32[2,6,1,512]{3,2,1,0:T(1,128)S(1)}, u32[]{:S(2)}, u32[]{:S(2)}) %collective-permute-start.37) | collective-permute-done | bytes 24608 | tf_op jit(solution)/shard_map/ppermute | solution.py:20
  290.2 3.8 %collective-permute-done.39 = f32[2,1,64,512]{3,2,1,0:T(8,128)} collective-permute-done((f32[2,1,64,512]{3,2,1,0:T(8,128)}, f32[2,1,64,512]{3,2,1,0:T(8,128)}, u32[]{:S(2)}, u32[]{:S(2)}) %collective-permute-start.39) | collective-permute-done | bytes 262176 | tf_op jit(solution)/shard_map/ppermute | solution.py:20
  (174 shorter events, 172.3 us)
Async XLA Ops:
  1.7 6.3 %collective-permute-start.1 = (f32[1,64,512]{2,1,0:T(8,128)S(1)}, f32[1,64,512]{2,1,0:T(8,128)S(1)}, u32[]{:S(2)}, u32[]{:S(2)}) collective-permute-start(f32[1,64,512]{2,1,0:T(8,128)S(1)} %get-tuple-element.63), channel_id=1, source_target_pairs={{0,4},{4,8},{8,12},{12,16},{16,20},{20,24},{24,28},{1,5},{5,9},{9,... | collective-permute-start | bytes 393224 | tf_op jit(solution)/shard_map/ppermute | solution.py:20
  13.2 6.5 %collective-permute-start.3 = (f32[6,1,512]{2,1,0:T(1,128)S(1)}, f32[6,1,512]{2,1,0:T(1,128)S(1)}, u32[]{:S(2)}, u32[]{:S(2)}) collective-permute-start(f32[6,1,512]{2,1,0:T(1,128)S(1)} %get-tuple-element.60), channel_id=1, source_target_pairs={{0,1},{1,2},{2,3},{4,5},{5,6},{6,7},{8,9},{9,10},{10,11},{12,13},{... | collective-permute-start | bytes 36872 | tf_op jit(solution)/shard_map/ppermute | solution.py:20
  22.4 6.2 %collective-permute-start.4 = (f32[2,1,64,512]{3,2,1,0:T(8,128)S(1)}, f32[2,1,64,512]{3,2,1,0:T(8,128)S(1)}, u32[]{:S(2)}, u32[]{:S(2)}) collective-permute-start(f32[2,1,64,512]{3,2,1,0:T(8,128)S(1)} %get-tuple-element.59), channel_id=1, source_target_pairs={{4,0},{8,4},{12,8},{16,12},{20,16},{24,20},{28,24},{5,1},{9,5},{13... | collective-permute-start | bytes 786440 | tf_op jit(solution)/shard_map/ppermute | solution.py:22
  24.8 7.7 %collective-permute-start.5 = (f32[2,1,64,512]{3,2,1,0:T(8,128)S(1)}, f32[2,1,64,512]{3,2,1,0:T(8,128)S(1)}, u32[]{:S(2)}, u32[]{:S(2)}) collective-permute-start(f32[2,1,64,512]{3,2,1,0:T(8,128)S(1)} %get-tuple-element.58), channel_id=1, source_target_pairs={{0,4},{4,8},{8,12},{12,16},{16,20},{20,24},{24,28},{1,5},{5,9},{9,... | collective-permute-start | bytes 786440 | tf_op jit(solution)/shard_map/ppermute | solution.py:20
  34.5 6.6 %collective-permute-start.7 = (f32[2,6,1,512]{3,2,1,0:T(1,128)S(1)}, f32[2,6,1,512]{3,2,1,0:T(1,128)S(1)}, u32[]{:S(2)}, u32[]{:S(2)}) collective-permute-start(f32[2,6,1,512]{3,2,1,0:T(1,128)S(1)} %get-tuple-element.42), channel_id=1, source_target_pairs={{0,1},{1,2},{2,3},{4,5},{5,6},{6,7},{8,9},{9,10},{10,11},{12,13},{... | collective-permute-start | bytes 73736 | tf_op jit(solution)/shard_map/ppermute | solution.py:20
  45.5 7.7 %collective-permute-start.9 = (f32[2,1,64,512]{3,2,1,0:T(8,128)S(1)}, f32[2,1,64,512]{3,2,1,0:T(8,128)S(1)}, u32[]{:S(2)}, u32[]{:S(2)}) collective-permute-start(f32[2,1,64,512]{3,2,1,0:T(8,128)S(1)} %get-tuple-element.56), channel_id=1, source_target_pairs={{0,4},{4,8},{8,12},{12,16},{16,20},{20,24},{24,28},{1,5},{5,9},{9,... | collective-permute-start | bytes 786440 | tf_op jit(solution)/shard_map/ppermute | solution.py:20
  55.2 6.6 %collective-permute-start.11 = (f32[2,6,1,512]{3,2,1,0:T(1,128)S(1)}, f32[2,6,1,512]{3,2,1,0:T(1,128)S(1)}, u32[]{:S(2)}, u32[]{:S(2)}) collective-permute-start(f32[2,6,1,512]{3,2,1,0:T(1,128)S(1)} %get-tuple-element.40), channel_id=1, source_target_pairs={{0,1},{1,2},{2,3},{4,5},{5,6},{6,7},{8,9},{9,10},{10,11},{12,13},{... | collective-permute-start | bytes 73736 | tf_op jit(solution)/shard_map/ppermute | solution.py:20
  83.8 7.5 %collective-permute-start.14 = (f32[2,1,64,512]{3,2,1,0:T(8,128)S(1)}, f32[2,1,64,512]{3,2,1,0:T(8,128)S(1)}, u32[]{:S(2)}, u32[]{:S(2)}) collective-permute-start(f32[2,1,64,512]{3,2,1,0:T(8,128)S(1)} %get-tuple-element.55), channel_id=1, source_target_pairs={{4,0},{8,4},{12,8},{16,12},{20,16},{24,20},{28,24},{5,1},{9,5},{13... | collective-permute-start | bytes 786440 | tf_op jit(solution)/shard_map/ppermute | solution.py:22
  87.4 7.7 %collective-permute-start.15 = (f32[2,1,64,512]{3,2,1,0:T(8,128)S(1)}, f32[2,1,64,512]{3,2,1,0:T(8,128)S(1)}, u32[]{:S(2)}, u32[]{:S(2)}) collective-permute-start(f32[2,1,64,512]{3,2,1,0:T(8,128)S(1)} %get-tuple-element.54), channel_id=1, source_target_pairs={{0,4},{4,8},{8,12},{12,16},{16,20},{20,24},{24,28},{1,5},{5,9},{9,... | collective-permute-start | bytes 786440 | tf_op jit(solution)/shard_map/ppermute | solution.py:20
  98.1 6.6 %collective-permute-start.17 = (f32[2,6,1,512]{3,2,1,0:T(1,128)S(1)}, f32[2,6,1,512]{3,2,1,0:T(1,128)S(1)}, u32[]{:S(2)}, u32[]{:S(2)}) collective-permute-start(f32[2,6,1,512]{3,2,1,0:T(1,128)S(1)} %get-tuple-element.38), channel_id=1, source_target_pairs={{0,1},{1,2},{2,3},{4,5},{5,6},{6,7},{8,9},{9,10},{10,11},{12,13},{... | collective-permute-start | bytes 73736 | tf_op jit(solution)/shard_map/ppermute | solution.py:20
  109.2 7.7 %collective-permute-start.19 = (f32[2,1,64,512]{3,2,1,0:T(8,128)S(1)}, f32[2,1,64,512]{3,2,1,0:T(8,128)S(1)}, u32[]{:S(2)}, u32[]{:S(2)}) collective-permute-start(f32[2,1,64,512]{3,2,1,0:T(8,128)S(1)} %get-tuple-element.52), channel_id=1, source_target_pairs={{0,4},{4,8},{8,12},{12,16},{16,20},{20,24},{24,28},{1,5},{5,9},{9,... | collective-permute-start | bytes 786440 | tf_op jit(solution)/shard_map/ppermute | solution.py:20
  119.9 6.6 %collective-permute-start.21 = (f32[2,6,1,512]{3,2,1,0:T(1,128)S(1)}, f32[2,6,1,512]{3,2,1,0:T(1,128)S(1)}, u32[]{:S(2)}, u32[]{:S(2)}) collective-permute-start(f32[2,6,1,512]{3,2,1,0:T(1,128)S(1)} %get-tuple-element.36), channel_id=1, source_target_pairs={{0,1},{1,2},{2,3},{4,5},{5,6},{6,7},{8,9},{9,10},{10,11},{12,13},{... | collective-permute-start | bytes 73736 | tf_op jit(solution)/shard_map/ppermute | solution.py:20
  171.7 6.3 %collective-permute-start.23 = (f32[1,512]{1,0:T(1,128)S(1)}, f32[1,512]{1,0:T(1,128)S(1)}, u32[]{:S(2)}, u32[]{:S(2)}) collective-permute-start(f32[1,512]{1,0:T(1,128)S(1)} %slice.583), channel_id=1, source_target_pairs={{4,0},{8,4},{12,8},{16,12},{20,16},{24,20},{28,24},{5,1},{9,5},{13... | collective-permute-start | bytes 6152 | tf_op jit(solution)/shard_map/ppermute | solution.py:32
  179.2 7.5 %collective-permute-start.24 = (f32[2,1,64,512]{3,2,1,0:T(8,128)S(1)}, f32[2,1,64,512]{3,2,1,0:T(8,128)S(1)}, u32[]{:S(2)}, u32[]{:S(2)}) collective-permute-start(f32[2,1,64,512]{3,2,1,0:T(8,128)S(1)} %get-tuple-element.51), channel_id=1, source_target_pairs={{4,0},{8,4},{12,8},{16,12},{20,16},{24,20},{28,24},{5,1},{9,5},{13... | collective-permute-start | bytes 786440 | tf_op jit(solution)/shard_map/ppermute | solution.py:22
  182.9 7.7 %collective-permute-start.25 = (f32[2,1,64,512]{3,2,1,0:T(8,128)S(1)}, f32[2,1,64,512]{3,2,1,0:T(8,128)S(1)}, u32[]{:S(2)}, u32[]{:S(2)}) collective-permute-start(f32[2,1,64,512]{3,2,1,0:T(8,128)S(1)} %get-tuple-element.50), channel_id=1, source_target_pairs={{0,4},{4,8},{8,12},{12,16},{16,20},{20,24},{24,28},{1,5},{5,9},{9,... | collective-permute-start | bytes 786440 | tf_op jit(solution)/shard_map/ppermute | solution.py:20
  194.7 6.6 %collective-permute-start.27 = (f32[2,6,1,512]{3,2,1,0:T(1,128)S(1)}, f32[2,6,1,512]{3,2,1,0:T(1,128)S(1)}, u32[]{:S(2)}, u32[]{:S(2)}) collective-permute-start(f32[2,6,1,512]{3,2,1,0:T(1,128)S(1)} %get-tuple-element.34), channel_id=1, source_target_pairs={{0,1},{1,2},{2,3},{4,5},{5,6},{6,7},{8,9},{9,10},{10,11},{12,13},{... | collective-permute-start | bytes 73736 | tf_op jit(solution)/shard_map/ppermute | solution.py:20
  205.7 7.7 %collective-permute-start.29 = (f32[2,1,64,512]{3,2,1,0:T(8,128)S(1)}, f32[2,1,64,512]{3,2,1,0:T(8,128)S(1)}, u32[]{:S(2)}, u32[]{:S(2)}) collective-permute-start(f32[2,1,64,512]{3,2,1,0:T(8,128)S(1)} %get-tuple-element.48), channel_id=1, source_target_pairs={{0,4},{4,8},{8,12},{12,16},{16,20},{20,24},{24,28},{1,5},{5,9},{9,... | collective-permute-start | bytes 786440 | tf_op jit(solution)/shard_map/ppermute | solution.py:20
  215.5 6.6 %collective-permute-start.31 = (f32[2,6,1,512]{3,2,1,0:T(1,128)S(1)}, f32[2,6,1,512]{3,2,1,0:T(1,128)S(1)}, u32[]{:S(2)}, u32[]{:S(2)}) collective-permute-start(f32[2,6,1,512]{3,2,1,0:T(1,128)S(1)} %get-tuple-element.32), channel_id=1, source_target_pairs={{0,1},{1,2},{2,3},{4,5},{5,6},{6,7},{8,9},{9,10},{10,11},{12,13},{... | collective-permute-start | bytes 73736 | tf_op jit(solution)/shard_map/ppermute | solution.py:20
  257.9 7.5 %collective-permute-start.34 = (f32[2,1,64,512]{3,2,1,0:T(8,128)S(1)}, f32[2,1,64,512]{3,2,1,0:T(8,128)S(1)}, u32[]{:S(2)}, u32[]{:S(2)}) collective-permute-start(f32[2,1,64,512]{3,2,1,0:T(8,128)S(1)} %get-tuple-element.47), channel_id=1, source_target_pairs={{4,0},{8,4},{12,8},{16,12},{20,16},{24,20},{28,24},{5,1},{9,5},{13... | collective-permute-start | bytes 786440 | tf_op jit(solution)/shard_map/ppermute | solution.py:22
  261.5 7.7 %collective-permute-start.35 = (f32[2,1,64,512]{3,2,1,0:T(8,128)S(1)}, f32[2,1,64,512]{3,2,1,0:T(8,128)S(1)}, u32[]{:S(2)}, u32[]{:S(2)}) collective-permute-start(f32[2,1,64,512]{3,2,1,0:T(8,128)S(1)} %get-tuple-element.46), channel_id=1, source_target_pairs={{0,4},{4,8},{8,12},{12,16},{16,20},{20,24},{24,28},{1,5},{5,9},{9,... | collective-permute-start | bytes 786440 | tf_op jit(solution)/shard_map/ppermute | solution.py:20
  272.3 6.6 %collective-permute-start.37 = (f32[2,6,1,512]{3,2,1,0:T(1,128)S(1)}, f32[2,6,1,512]{3,2,1,0:T(1,128)S(1)}, u32[]{:S(2)}, u32[]{:S(2)}) collective-permute-start(f32[2,6,1,512]{3,2,1,0:T(1,128)S(1)} %get-tuple-element.30), channel_id=1, source_target_pairs={{0,1},{1,2},{2,3},{4,5},{5,6},{6,7},{8,9},{9,10},{10,11},{12,13},{... | collective-permute-start | bytes 73736 | tf_op jit(solution)/shard_map/ppermute | solution.py:20
  286.0 8.0 %collective-permute-start.39 = (f32[2,1,64,512]{3,2,1,0:T(8,128)}, f32[2,1,64,512]{3,2,1,0:T(8,128)}, u32[]{:S(2)}, u32[]{:S(2)}) collective-permute-start(f32[2,1,64,512]{3,2,1,0:T(8,128)} %get-tuple-element.44), channel_id=1, source_target_pairs={{0,4},{4,8},{8,12},{12,16},{16,20},{20,24},{24,28},{1,5},{5,9},{9,... | collective-permute-start | bytes 786440 | tf_op jit(solution)/shard_map/ppermute | solution.py:20
  295.1 6.6 %collective-permute-start.40 = (f32[2,6,1,512]{3,2,1,0:T(1,128)S(1)}, f32[2,6,1,512]{3,2,1,0:T(1,128)S(1)}, u32[]{:S(2)}, u32[]{:S(2)}) collective-permute-start(f32[2,6,1,512]{3,2,1,0:T(1,128)S(1)} %get-tuple-element.29), channel_id=1, source_target_pairs={{1,0},{2,1},{3,2},{5,4},{6,5},{7,6},{9,8},{10,9},{11,10},{13,12},{... | collective-permute-start | bytes 73736 | tf_op jit(solution)/shard_map/ppermute | solution.py:22
  298.1 6.6 %collective-permute-start.41 = (f32[2,6,1,512]{3,2,1,0:T(1,128)S(1)}, f32[2,6,1,512]{3,2,1,0:T(1,128)S(1)}, u32[]{:S(2)}, u32[]{:S(2)}) collective-permute-start(f32[2,6,1,512]{3,2,1,0:T(1,128)S(1)} %get-tuple-element.28), channel_id=1, source_target_pairs={{0,1},{1,2},{2,3},{4,5},{5,6},{6,7},{8,9},{9,10},{10,11},{12,13},{... | collective-permute-start | bytes 73736 | tf_op jit(solution)/shard_map/ppermute | solution.py:20
  (34 other events, 295.4 us)
where the time goes:
time: 312 us; the launch traced here: 310 us
  starting transfers between devices  112 us (36%)
  waiting for transfers between devices  89.3 us (29%)
  blocking collectives  61.2 us (20%)
  other arithmetic  32.4 us (10%)
  local copies, waits for them, and re-layouts  6.4 us (2%)
  between operations  5.48 us (2%)
  matrix products  3.36 us (1%)
    ppermute x18, waiting for transfers between devices, with_halo(): lax.ppermute(tail, axis, [(i, (i + 1) % count) for i in range(ends)])  62.2 us
    ppermute x18, starting transfers between devices, with_halo(): lax.ppermute(head, axis, [((i + 1) % count, i) for i in range(ends)])  49.8 us
    ppermute x18, starting transfers between devices, with_halo(): lax.ppermute(tail, axis, [(i, (i + 1) % count) for i in range(ends)])  47 us
    psum x3, blocking collectives, total(): return lax.psum(value, 'slab')  36.2 us
    psum x3, blocking collectives, diverge(): return lax.psum(ordered, 'cross')  25.1 us
    add x8, other arithmetic, velocity_solve(): solved = solved + change  15.6 us
    ppermute x6, starting transfers between devices, passed_along(): return lax.ppermute(block, axis, route)  15.1 us
    ppermute x18, waiting for transfers between devices, with_halo(): lax.ppermute(head, axis, [((i + 1) % count, i) for i in range(ends)])  14.5 us
  transfers between devices with their start and end apart: 42, of which 33 were waited for; matrix products, arithmetic and copies ran while one was open for 1% of the time, Pallas kernels for 0%

commit v1 on v0

--- a/solution.py
+++ b/solution.py
@@ -88,7 +88,12 @@
     behind = jnp.pad(col_z[:, :-1], ((0, 0), (1, 0)))
     local = col_x - below + col_z - behind
     ordered = jnp.dot(local, onehot, precision=lax.Precision.HIGHEST)
-    return lax.psum(ordered, "cross")
+
+    def raise_columns(bus_axis, frame_in):
+        local_now = jax.lax.all_gather(frame_in, bus_axis).sum(axis=0)
+        return local_now
+
+    return raise_columns("cross", ordered)
 
 
 def gradient(press, onehot, ny):

time: 312 us -> 308 us (0.987)
    psum x3 -> x0, blocking collectives: 25.1 us -> none  [diverge(): return lax.psum(ordered, 'cross')]
    all_gather x0 -> x3, blocking collectives: none -> 23.3 us  [raise_columns(): local_now = jax.lax.all_gather(frame_in, bus_axis).sum(axis=0)]
where the time goes in v1:
time: 308 us; the launch traced here: 307 us
  starting transfers between devices  112 us (36%)
  waiting for transfers between devices  87.4 us (28%)
  blocking collectives  59.5 us (19%)
  other arithmetic  32.4 us (11%)
  local copies, waits for them, and re-layouts  6.4 us (2%)
  between operations  5.47 us (2%)
  matrix products  3.36 us (1%)
    ppermute x18, waiting for transfers between devices, with_halo(): lax.ppermute(tail, axis, [(i, (i + 1) % count) for i in range(ends)])  60.5 us
    ppermute x18, starting transfers between devices, with_halo(): lax.ppermute(tail, axis, [(i, (i + 1) % count) for i in range(ends)])  48.7 us
    ppermute x18, starting transfers between devices, with_halo(): lax.ppermute(head, axis, [((i + 1) % count, i) for i in range(ends)])  48.1 us
    psum x3, blocking collectives, total(): return lax.psum(value, 'slab')  36.2 us
    all_gather x3, blocking collectives, raise_columns(): local_now = jax.lax.all_gather(frame_in, bus_axis).sum(axis=0)  23.3 us
    add x8, other arithmetic, velocity_solve(): solved = solved + change  15.6 us
    ppermute x6, starting transfers between devices, passed_along(): return lax.ppermute(block, axis, route)  15.3 us
    ppermute x18, waiting for transfers between devices, with_halo(): lax.ppermute(head, axis, [((i + 1) % count, i) for i in range(ends)])  14.5 us
  transfers between devices with their start and end apart: 42, of which 33 were waited for; matrix products, arithmetic and copies ran while one was open for 1% of the time, Pallas kernels for 0%

profile of v1, /device:TPU:12, one launch (start us, length us, event | category | flops | bytes accessed | tf_op | source)
XLA Modules:
  0.0 306.7 jit_solution(4125909231881144252)
XLA Ops:
  15.7 4.0 %collective-permute-done.3 = f32[6,1,512]{2,1,0:T(1,128)S(1)} collective-permute-done((f32[6,1,512]{2,1,0:T(1,128)S(1)}, f32[6,1,512]{2,1,0:T(1,128)S(1)}, u32[]{:S(2)}, u32[]{:S(2)}) %collective-permute-start.3) | collective-permute-done | bytes 12320 | tf_op jit(solution)/shard_map/ppermute | solution.py:20
  28.7 3.8 %collective-permute-done.5 = f32[2,1,64,512]{3,2,1,0:T(8,128)S(1)} collective-permute-done((f32[2,1,64,512]{3,2,1,0:T(8,128)S(1)}, f32[2,1,64,512]{3,2,1,0:T(8,128)S(1)}, u32[]{:S(2)}, u32[]{:S(2)}) %collective-permute-start.5) | collective-permute-done | bytes 262176 | tf_op jit(solution)/shard_map/ppermute | solution.py:20
  34.5 3.9 %collective-permute-start.7 = (f32[2,6,1,512]{3,2,1,0:T(1,128)S(1)}, f32[2,6,1,512]{3,2,1,0:T(1,128)S(1)}, u32[]{:S(2)}, u32[]{:S(2)}) collective-permute-start(f32[2,6,1,512]{3,2,1,0:T(1,128)S(1)} %get-tuple-element.42), channel_id=1, source_target_pairs={{0,1},{1,2},{2,3},{4,5},{5,6},{6,7},{8,9},{9,10},{10,11},{12,13},{... | collective-permute-start | bytes 73736 | tf_op jit(solution)/shard_map/ppermute | solution.py:20
  49.4 3.8 %collective-permute-done.9 = f32[2,1,64,512]{3,2,1,0:T(8,128)S(1)} collective-permute-done((f32[2,1,64,512]{3,2,1,0:T(8,128)S(1)}, f32[2,1,64,512]{3,2,1,0:T(8,128)S(1)}, u32[]{:S(2)}, u32[]{:S(2)}) %collective-permute-start.9) | collective-permute-done | bytes 262176 | tf_op jit(solution)/shard_map/ppermute | solution.py:20
  55.2 3.9 %collective-permute-start.11 = (f32[2,6,1,512]{3,2,1,0:T(1,128)S(1)}, f32[2,6,1,512]{3,2,1,0:T(1,128)S(1)}, u32[]{:S(2)}, u32[]{:S(2)}) collective-permute-start(f32[2,6,1,512]{3,2,1,0:T(1,128)S(1)} %get-tuple-element.40), channel_id=1, source_target_pairs={{0,1},{1,2},{2,3},{4,5},{5,6},{6,7},{8,9},{9,10},{10,11},{12,13},{... | collective-permute-start | bytes 73736 | tf_op jit(solution)/shard_map/ppermute | solution.py:20
  70.0 7.8 %all-gather.3 = f32[4,4,512]{2,1,0:T(4,128)S(1)} all-gather(f32[1,4,512]{2,1,0:T(4,128)S(1)} %convolution_bitcast_fusion.2), channel_id=2, replica_groups=mesh['slab'=8,'cross'=4] {'cross'}, dimensions={0}, use_global_device_ids=true | all-gather | bytes 40960 | tf_op jit(solution)/shard_map/all_gather | solution.py:93
  90.4 3.8 %collective-permute-done.15 = f32[2,1,64,512]{3,2,1,0:T(8,128)S(1)} collective-permute-done((f32[2,1,64,512]{3,2,1,0:T(8,128)S(1)}, f32[2,1,64,512]{3,2,1,0:T(8,128)S(1)}, u32[]{:S(2)}, u32[]{:S(2)}) %collective-permute-start.15) | collective-permute-done | bytes 262176 | tf_op jit(solution)/shard_map/ppermute | solution.py:20
  100.2 4.1 %collective-permute-done.17 = f32[2,6,1,512]{3,2,1,0:T(1,128)S(1)} collective-permute-done((f32[2,6,1,512]{3,2,1,0:T(1,128)S(1)}, f32[2,6,1,512]{3,2,1,0:T(1,128)S(1)}, u32[]{:S(2)}, u32[]{:S(2)}) %collective-permute-start.17) | collective-permute-done | bytes 24608 | tf_op jit(solution)/shard_map/ppermute | solution.py:20
  112.7 3.8 %collective-permute-done.19 = f32[2,1,64,512]{3,2,1,0:T(8,128)S(1)} collective-permute-done((f32[2,1,64,512]{3,2,1,0:T(8,128)S(1)}, f32[2,1,64,512]{3,2,1,0:T(8,128)S(1)}, u32[]{:S(2)}, u32[]{:S(2)}) %collective-permute-start.19) | collective-permute-done | bytes 262176 | tf_op jit(solution)/shard_map/ppermute | solution.py:20
  118.5 3.9 %collective-permute-start.21 = (f32[2,6,1,512]{3,2,1,0:T(1,128)S(1)}, f32[2,6,1,512]{3,2,1,0:T(1,128)S(1)}, u32[]{:S(2)}, u32[]{:S(2)}) collective-permute-start(f32[2,6,1,512]{3,2,1,0:T(1,128)S(1)} %get-tuple-element.36), channel_id=1, source_target_pairs={{0,1},{1,2},{2,3},{4,5},{5,6},{6,7},{8,9},{9,10},{10,11},{12,13},{... | collective-permute-start | bytes 73736 | tf_op jit(solution)/shard_map/ppermute | solution.py:20
  133.1 7.8 %all-gather.4 = f32[4,4,512]{2,1,0:T(4,128)S(1)} all-gather(f32[1,4,512]{2,1,0:T(4,128)S(1)} %convolution_bitcast_fusion.1), channel_id=3, replica_groups=mesh['slab'=8,'cross'=4] {'cross'}, dimensions={0}, use_global_device_ids=true | all-gather | bytes 40960 | tf_op jit(solution)/shard_map/all_gather | solution.py:93
  141.6 10.6 %all-reduce.15 = (f32[]{:T(128)}, f32[]{:T(128)}) all-reduce(f32[]{:T(128)} %get-tuple-element.9, f32[]{:T(128)} %get-tuple-element.8), channel_id=1, replica_groups=mesh['slab'=8,'cross'=4] {'slab'}, use_global_device_ids=true, to_apply=%region_4.5 | all-reduce | flops 2 | bytes 16 | tf_op jit(solution)/shard_map/psum | solution.py:109
  154.1 14.3 %psum.30 = f32[]{:T(128)} all-reduce(f32[]{:T(128)} %multiply_reduce_fusion.1), channel_id=1, replica_groups=mesh['slab'=8,'cross'=4] {'slab'}, use_global_device_ids=true, to_apply=%region_11.12 | all-reduce | flops 1 | bytes 8 | tf_op jit(solution)/shard_map/psum | solution.py:109
  170.3 5.0 %collective-permute-start.23 = (f32[1,512]{1,0:T(1,128)S(1)}, f32[1,512]{1,0:T(1,128)S(1)}, u32[]{:S(2)}, u32[]{:S(2)}) collective-permute-start(f32[1,512]{1,0:T(1,128)S(1)} %slice.583), channel_id=1, source_target_pairs={{4,0},{8,4},{12,8},{16,12},{20,16},{24,20},{28,24},{5,1},{9,5},{13... | collective-permute-start | bytes 6152 | tf_op jit(solution)/shard_map/ppermute | solution.py:32
  185.3 3.8 %collective-permute-done.25 = f32[2,1,64,512]{3,2,1,0:T(8,128)S(1)} collective-permute-done((f32[2,1,64,512]{3,2,1,0:T(8,128)S(1)}, f32[2,1,64,512]{3,2,1,0:T(8,128)S(1)}, u32[]{:S(2)}, u32[]{:S(2)}) %collective-permute-start.25) | collective-permute-done | bytes 262176 | tf_op jit(solution)/shard_map/ppermute | solution.py:20
  195.2 4.1 %collective-permute-done.27 = f32[2,6,1,512]{3,2,1,0:T(1,128)S(1)} collective-permute-done((f32[2,6,1,512]{3,2,1,0:T(1,128)S(1)}, f32[2,6,1,512]{3,2,1,0:T(1,128)S(1)}, u32[]{:S(2)}, u32[]{:S(2)}) %collective-permute-start.27) | collective-permute-done | bytes 24608 | tf_op jit(solution)/shard_map/ppermute | solution.py:20
  207.6 3.8 %collective-permute-done.29 = f32[2,1,64,512]{3,2,1,0:T(8,128)S(1)} collective-permute-done((f32[2,1,64,512]{3,2,1,0:T(8,128)S(1)}, f32[2,1,64,512]{3,2,1,0:T(8,128)S(1)}, u32[]{:S(2)}, u32[]{:S(2)}) %collective-permute-start.29) | collective-permute-done | bytes 262176 | tf_op jit(solution)/shard_map/ppermute | solution.py:20
  213.4 3.9 %collective-permute-start.31 = (f32[2,6,1,512]{3,2,1,0:T(1,128)S(1)}, f32[2,6,1,512]{3,2,1,0:T(1,128)S(1)}, u32[]{:S(2)}, u32[]{:S(2)}) collective-permute-start(f32[2,6,1,512]{3,2,1,0:T(1,128)S(1)} %get-tuple-element.32), channel_id=1, source_target_pairs={{0,1},{1,2},{2,3},{4,5},{5,6},{6,7},{8,9},{9,10},{10,11},{12,13},{... | collective-permute-start | bytes 73736 | tf_op jit(solution)/shard_map/ppermute | solution.py:20
  228.1 7.8 %all-gather.5 = f32[4,4,512]{2,1,0:T(4,128)S(1)} all-gather(f32[1,4,512]{2,1,0:T(4,128)S(1)} %convolution_bitcast_fusion), channel_id=4, replica_groups=mesh['slab'=8,'cross'=4] {'cross'}, dimensions={0}, use_global_device_ids=true | all-gather | bytes 40960 | tf_op jit(solution)/shard_map/all_gather | solution.py:93
  236.5 11.2 %psum.31 = f32[]{:T(128)} all-reduce(f32[]{:T(128)} %multiply_reduce_fusion), channel_id=1, replica_groups=mesh['slab'=8,'cross'=4] {'slab'}, use_global_device_ids=true, to_apply=%region_16.17 | all-reduce | flops 1 | bytes 8 | tf_op jit(solution)/shard_map/psum | solution.py:109
  262.5 3.8 %collective-permute-done.35 = f32[2,1,64,512]{3,2,1,0:T(8,128)S(1)} collective-permute-done((f32[2,1,64,512]{3,2,1,0:T(8,128)S(1)}, f32[2,1,64,512]{3,2,1,0:T(8,128)S(1)}, u32[]{:S(2)}, u32[]{:S(2)}) %collective-permute-start.35) | collective-permute-done | bytes 262176 | tf_op jit(solution)/shard_map/ppermute | solution.py:20
  272.4 4.1 %collective-permute-done.37 = f32[2,6,1,512]{3,2,1,0:T(1,128)S(1)} collective-permute-done((f32[2,6,1,512]{3,2,1,0:T(1,128)S(1)}, f32[2,6,1,512]{3,2,1,0:T(1,128)S(1)}, u32[]{:S(2)}, u32[]{:S(2)}) %collective-permute-start.37) | collective-permute-done | bytes 24608 | tf_op jit(solution)/shard_map/ppermute | solution.py:20
  287.8 3.8 %collective-permute-done.39 = f32[2,1,64,512]{3,2,1,0:T(8,128)} collective-permute-done((f32[2,1,64,512]{3,2,1,0:T(8,128)}, f32[2,1,64,512]{3,2,1,0:T(8,128)}, u32[]{:S(2)}, u32[]{:S(2)}) %collective-permute-start.39) | collective-permute-done | bytes 262176 | tf_op jit(solution)/shard_map/ppermute | solution.py:20
  294.7 3.9 %collective-permute-start.41 = (f32[2,6,1,512]{3,2,1,0:T(1,128)S(1)}, f32[2,6,1,512]{3,2,1,0:T(1,128)S(1)}, u32[]{:S(2)}, u32[]{:S(2)}) collective-permute-start(f32[2,6,1,512]{3,2,1,0:T(1,128)S(1)} %get-tuple-element.28), channel_id=1, source_target_pairs={{0,1},{1,2},{2,3},{4,5},{5,6},{6,7},{8,9},{9,10},{10,11},{12,13},{... | collective-permute-start | bytes 73736 | tf_op jit(solution)/shard_map/ppermute | solution.py:20
  (177 shorter events, 170.2 us)
Async XLA Ops:
  1.7 6.3 %collective-permute-start.1 = (f32[1,64,512]{2,1,0:T(8,128)S(1)}, f32[1,64,512]{2,1,0:T(8,128)S(1)}, u32[]{:S(2)}, u32[]{:S(2)}) collective-permute-start(f32[1,64,512]{2,1,0:T(8,128)S(1)} %get-tuple-element.63), channel_id=1, source_target_pairs={{0,4},{4,8},{8,12},{12,16},{16,20},{20,24},{24,28},{1,5},{5,9},{9,... | collective-permute-start | bytes 393224 | tf_op jit(solution)/shard_map/ppermute | solution.py:20
  13.2 6.5 %collective-permute-start.3 = (f32[6,1,512]{2,1,0:T(1,128)S(1)}, f32[6,1,512]{2,1,0:T(1,128)S(1)}, u32[]{:S(2)}, u32[]{:S(2)}) collective-permute-start(f32[6,1,512]{2,1,0:T(1,128)S(1)} %get-tuple-element.60), channel_id=1, source_target_pairs={{0,1},{1,2},{2,3},{4,5},{5,6},{6,7},{8,9},{9,10},{10,11},{12,13},{... | collective-permute-start | bytes 36872 | tf_op jit(solution)/shard_map/ppermute | solution.py:20
  22.4 6.2 %collective-permute-start.4 = (f32[2,1,64,512]{3,2,1,0:T(8,128)S(1)}, f32[2,1,64,512]{3,2,1,0:T(8,128)S(1)}, u32[]{:S(2)}, u32[]{:S(2)}) collective-permute-start(f32[2,1,64,512]{3,2,1,0:T(8,128)S(1)} %get-tuple-element.59), channel_id=1, source_target_pairs={{4,0},{8,4},{12,8},{16,12},{20,16},{24,20},{28,24},{5,1},{9,5},{13... | collective-permute-start | bytes 786440 | tf_op jit(solution)/shard_map/ppermute | solution.py:22
  24.8 7.7 %collective-permute-start.5 = (f32[2,1,64,512]{3,2,1,0:T(8,128)S(1)}, f32[2,1,64,512]{3,2,1,0:T(8,128)S(1)}, u32[]{:S(2)}, u32[]{:S(2)}) collective-permute-start(f32[2,1,64,512]{3,2,1,0:T(8,128)S(1)} %get-tuple-element.58), channel_id=1, source_target_pairs={{0,4},{4,8},{8,12},{12,16},{16,20},{20,24},{24,28},{1,5},{5,9},{9,... | collective-permute-start | bytes 786440 | tf_op jit(solution)/shard_map/ppermute | solution.py:20
  34.5 6.6 %collective-permute-start.7 = (f32[2,6,1,512]{3,2,1,0:T(1,128)S(1)}, f32[2,6,1,512]{3,2,1,0:T(1,128)S(1)}, u32[]{:S(2)}, u32[]{:S(2)}) collective-permute-start(f32[2,6,1,512]{3,2,1,0:T(1,128)S(1)} %get-tuple-element.42), channel_id=1, source_target_pairs={{0,1},{1,2},{2,3},{4,5},{5,6},{6,7},{8,9},{9,10},{10,11},{12,13},{... | collective-permute-start | bytes 73736 | tf_op jit(solution)/shard_map/ppermute | solution.py:20
  45.5 7.7 %collective-permute-start.9 = (f32[2,1,64,512]{3,2,1,0:T(8,128)S(1)}, f32[2,1,64,512]{3,2,1,0:T(8,128)S(1)}, u32[]{:S(2)}, u32[]{:S(2)}) collective-permute-start(f32[2,1,64,512]{3,2,1,0:T(8,128)S(1)} %get-tuple-element.56), channel_id=1, source_target_pairs={{0,4},{4,8},{8,12},{12,16},{16,20},{20,24},{24,28},{1,5},{5,9},{9,... | collective-permute-start | bytes 786440 | tf_op jit(solution)/shard_map/ppermute | solution.py:20
  55.2 6.6 %collective-permute-start.11 = (f32[2,6,1,512]{3,2,1,0:T(1,128)S(1)}, f32[2,6,1,512]{3,2,1,0:T(1,128)S(1)}, u32[]{:S(2)}, u32[]{:S(2)}) collective-permute-start(f32[2,6,1,512]{3,2,1,0:T(1,128)S(1)} %get-tuple-element.40), channel_id=1, source_target_pairs={{0,1},{1,2},{2,3},{4,5},{5,6},{6,7},{8,9},{9,10},{10,11},{12,13},{... | collective-permute-start | bytes 73736 | tf_op jit(solution)/shard_map/ppermute | solution.py:20
  82.9 7.5 %collective-permute-start.14 = (f32[2,1,64,512]{3,2,1,0:T(8,128)S(1)}, f32[2,1,64,512]{3,2,1,0:T(8,128)S(1)}, u32[]{:S(2)}, u32[]{:S(2)}) collective-permute-start(f32[2,1,64,512]{3,2,1,0:T(8,128)S(1)} %get-tuple-element.55), channel_id=1, source_target_pairs={{4,0},{8,4},{12,8},{16,12},{20,16},{24,20},{28,24},{5,1},{9,5},{13... | collective-permute-start | bytes 786440 | tf_op jit(solution)/shard_map/ppermute | solution.py:22
  86.5 7.7 %collective-permute-start.15 = (f32[2,1,64,512]{3,2,1,0:T(8,128)S(1)}, f32[2,1,64,512]{3,2,1,0:T(8,128)S(1)}, u32[]{:S(2)}, u32[]{:S(2)}) collective-permute-start(f32[2,1,64,512]{3,2,1,0:T(8,128)S(1)} %get-tuple-element.54), channel_id=1, source_target_pairs={{0,4},{4,8},{8,12},{12,16},{16,20},{20,24},{24,28},{1,5},{5,9},{9,... | collective-permute-start | bytes 786440 | tf_op jit(solution)/shard_map/ppermute | solution.py:20
  97.8 6.6 %collective-permute-start.17 = (f32[2,6,1,512]{3,2,1,0:T(1,128)S(1)}, f32[2,6,1,512]{3,2,1,0:T(1,128)S(1)}, u32[]{:S(2)}, u32[]{:S(2)}) collective-permute-start(f32[2,6,1,512]{3,2,1,0:T(1,128)S(1)} %get-tuple-element.38), channel_id=1, source_target_pairs={{0,1},{1,2},{2,3},{4,5},{5,6},{6,7},{8,9},{9,10},{10,11},{12,13},{... | collective-permute-start | bytes 73736 | tf_op jit(solution)/shard_map/ppermute | solution.py:20
  108.8 7.7 %collective-permute-start.19 = (f32[2,1,64,512]{3,2,1,0:T(8,128)S(1)}, f32[2,1,64,512]{3,2,1,0:T(8,128)S(1)}, u32[]{:S(2)}, u32[]{:S(2)}) collective-permute-start(f32[2,1,64,512]{3,2,1,0:T(8,128)S(1)} %get-tuple-element.52), channel_id=1, source_target_pairs={{0,4},{4,8},{8,12},{12,16},{16,20},{20,24},{24,28},{1,5},{5,9},{9,... | collective-permute-start | bytes 786440 | tf_op jit(solution)/shard_map/ppermute | solution.py:20
  118.5 6.6 %collective-permute-start.21 = (f32[2,6,1,512]{3,2,1,0:T(1,128)S(1)}, f32[2,6,1,512]{3,2,1,0:T(1,128)S(1)}, u32[]{:S(2)}, u32[]{:S(2)}) collective-permute-start(f32[2,6,1,512]{3,2,1,0:T(1,128)S(1)} %get-tuple-element.36), channel_id=1, source_target_pairs={{0,1},{1,2},{2,3},{4,5},{5,6},{6,7},{8,9},{9,10},{10,11},{12,13},{... | collective-permute-start | bytes 73736 | tf_op jit(solution)/shard_map/ppermute | solution.py:20
  170.3 6.3 %collective-permute-start.23 = (f32[1,512]{1,0:T(1,128)S(1)}, f32[1,512]{1,0:T(1,128)S(1)}, u32[]{:S(2)}, u32[]{:S(2)}) collective-permute-start(f32[1,512]{1,0:T(1,128)S(1)} %slice.583), channel_id=1, source_target_pairs={{4,0},{8,4},{12,8},{16,12},{20,16},{24,20},{28,24},{5,1},{9,5},{13... | collective-permute-start | bytes 6152 | tf_op jit(solution)/shard_map/ppermute | solution.py:32
  177.8 7.5 %collective-permute-start.24 = (f32[2,1,64,512]{3,2,1,0:T(8,128)S(1)}, f32[2,1,64,512]{3,2,1,0:T(8,128)S(1)}, u32[]{:S(2)}, u32[]{:S(2)}) collective-permute-start(f32[2,1,64,512]{3,2,1,0:T(8,128)S(1)} %get-tuple-element.51), channel_id=1, source_target_pairs={{4,0},{8,4},{12,8},{16,12},{20,16},{24,20},{28,24},{5,1},{9,5},{13... | collective-permute-start | bytes 786440 | tf_op jit(solution)/shard_map/ppermute | solution.py:22
  181.5 7.7 %collective-permute-start.25 = (f32[2,1,64,512]{3,2,1,0:T(8,128)S(1)}, f32[2,1,64,512]{3,2,1,0:T(8,128)S(1)}, u32[]{:S(2)}, u32[]{:S(2)}) collective-permute-start(f32[2,1,64,512]{3,2,1,0:T(8,128)S(1)} %get-tuple-element.50), channel_id=1, source_target_pairs={{0,4},{4,8},{8,12},{12,16},{16,20},{20,24},{24,28},{1,5},{5,9},{9,... | collective-permute-start | bytes 786440 | tf_op jit(solution)/shard_map/ppermute | solution.py:20
  192.7 6.6 %collective-permute-start.27 = (f32[2,6,1,512]{3,2,1,0:T(1,128)S(1)}, f32[2,6,1,512]{3,2,1,0:T(1,128)S(1)}, u32[]{:S(2)}, u32[]{:S(2)}) collective-permute-start(f32[2,6,1,512]{3,2,1,0:T(1,128)S(1)} %get-tuple-element.34), channel_id=1, source_target_pairs={{0,1},{1,2},{2,3},{4,5},{5,6},{6,7},{8,9},{9,10},{10,11},{12,13},{... | collective-permute-start | bytes 73736 | tf_op jit(solution)/shard_map/ppermute | solution.py:20
  203.8 7.7 %collective-permute-start.29 = (f32[2,1,64,512]{3,2,1,0:T(8,128)S(1)}, f32[2,1,64,512]{3,2,1,0:T(8,128)S(1)}, u32[]{:S(2)}, u32[]{:S(2)}) collective-permute-start(f32[2,1,64,512]{3,2,1,0:T(8,128)S(1)} %get-tuple-element.48), channel_id=1, source_target_pairs={{0,4},{4,8},{8,12},{12,16},{16,20},{20,24},{24,28},{1,5},{5,9},{9,... | collective-permute-start | bytes 786440 | tf_op jit(solution)/shard_map/ppermute | solution.py:20
  213.4 6.6 %collective-permute-start.31 = (f32[2,6,1,512]{3,2,1,0:T(1,128)S(1)}, f32[2,6,1,512]{3,2,1,0:T(1,128)S(1)}, u32[]{:S(2)}, u32[]{:S(2)}) collective-permute-start(f32[2,6,1,512]{3,2,1,0:T(1,128)S(1)} %get-tuple-element.32), channel_id=1, source_target_pairs={{0,1},{1,2},{2,3},{4,5},{5,6},{6,7},{8,9},{9,10},{10,11},{12,13},{... | collective-permute-start | bytes 73736 | tf_op jit(solution)/shard_map/ppermute | solution.py:20
  255.0 7.5 %collective-permute-start.34 = (f32[2,1,64,512]{3,2,1,0:T(8,128)S(1)}, f32[2,1,64,512]{3,2,1,0:T(8,128)S(1)}, u32[]{:S(2)}, u32[]{:S(2)}) collective-permute-start(f32[2,1,64,512]{3,2,1,0:T(8,128)S(1)} %get-tuple-element.47), channel_id=1, source_target_pairs={{4,0},{8,4},{12,8},{16,12},{20,16},{24,20},{28,24},{5,1},{9,5},{13... | collective-permute-start | bytes 786440 | tf_op jit(solution)/shard_map/ppermute | solution.py:22
  258.7 7.7 %collective-permute-start.35 = (f32[2,1,64,512]{3,2,1,0:T(8,128)S(1)}, f32[2,1,64,512]{3,2,1,0:T(8,128)S(1)}, u32[]{:S(2)}, u32[]{:S(2)}) collective-permute-start(f32[2,1,64,512]{3,2,1,0:T(8,128)S(1)} %get-tuple-element.46), channel_id=1, source_target_pairs={{0,4},{4,8},{8,12},{12,16},{16,20},{20,24},{24,28},{1,5},{5,9},{9,... | collective-permute-start | bytes 786440 | tf_op jit(solution)/shard_map/ppermute | solution.py:20
  269.9 6.6 %collective-permute-start.37 = (f32[2,6,1,512]{3,2,1,0:T(1,128)S(1)}, f32[2,6,1,512]{3,2,1,0:T(1,128)S(1)}, u32[]{:S(2)}, u32[]{:S(2)}) collective-permute-start(f32[2,6,1,512]{3,2,1,0:T(1,128)S(1)} %get-tuple-element.30), channel_id=1, source_target_pairs={{0,1},{1,2},{2,3},{4,5},{5,6},{6,7},{8,9},{9,10},{10,11},{12,13},{... | collective-permute-start | bytes 73736 | tf_op jit(solution)/shard_map/ppermute | solution.py:20
  283.6 8.0 %collective-permute-start.39 = (f32[2,1,64,512]{3,2,1,0:T(8,128)}, f32[2,1,64,512]{3,2,1,0:T(8,128)}, u32[]{:S(2)}, u32[]{:S(2)}) collective-permute-start(f32[2,1,64,512]{3,2,1,0:T(8,128)} %get-tuple-element.44), channel_id=1, source_target_pairs={{0,4},{4,8},{8,12},{12,16},{16,20},{20,24},{24,28},{1,5},{5,9},{9,... | collective-permute-start | bytes 786440 | tf_op jit(solution)/shard_map/ppermute | solution.py:20
  292.7 6.6 %collective-permute-start.40 = (f32[2,6,1,512]{3,2,1,0:T(1,128)S(1)}, f32[2,6,1,512]{3,2,1,0:T(1,128)S(1)}, u32[]{:S(2)}, u32[]{:S(2)}) collective-permute-start(f32[2,6,1,512]{3,2,1,0:T(1,128)S(1)} %get-tuple-element.29), channel_id=1, source_target_pairs={{1,0},{2,1},{3,2},{5,4},{6,5},{7,6},{9,8},{10,9},{11,10},{13,12},{... | collective-permute-start | bytes 73736 | tf_op jit(solution)/shard_map/ppermute | solution.py:22
  294.7 6.6 %collective-permute-start.41 = (f32[2,6,1,512]{3,2,1,0:T(1,128)S(1)}, f32[2,6,1,512]{3,2,1,0:T(1,128)S(1)}, u32[]{:S(2)}, u32[]{:S(2)}) collective-permute-start(f32[2,6,1,512]{3,2,1,0:T(1,128)S(1)} %get-tuple-element.28), channel_id=1, source_target_pairs={{0,1},{1,2},{2,3},{4,5},{5,6},{6,7},{8,9},{9,10},{10,11},{12,13},{... | collective-permute-start | bytes 73736 | tf_op jit(solution)/shard_map/ppermute | solution.py:20
  (34 other events, 292.4 us)
